TPU v7x, 32 devices: a whole 2x2x4 slice. The times are simulated.
32 devices in a mesh: user: 8 (over y, x, core), item: 4 (over z).
Axes of the slice: x: 2, y: 2, z: 4, core: 2. Of those that a mesh axis runs over, the one named last changes fastest.
Arguments:
- tokens: bfloat16 [16384, 1024], P(('user', 'item')), may hold values from -6 to 6
- lengths: int32 [32, 8], P(('user', 'item')), may hold values from 1 to 64, as said below
- destination: int32 [32, 8], P(('user', 'item')), may hold values from 0 to 7, as said below
- worker_offset: int32 [32, 8], P(('user', 'item')), may hold values from 0 to 255
- positives: int32 [16384], P(('user', 'item')), may hold values from 0 to 1023, as said below
- negatives: int32 [4, 256], replicated, may hold values from 0 to 1023, as said below
- table: bfloat16 [1024, 1024], P('item'), may hold values from -6 to 6
- in_gain: float32 [1024], replicated, may hold values from 0.1 to 1.9
- w_uvqk: bfloat16 [1024, 2048], P('item'), may hold values from -0.1875 to 0.1875
- out_gain: float32 [512], replicated, may hold values from 0.1 to 1.9
- w_out: bfloat16 [512, 1024], P(None, 'item'), may hold values from -0.25 to 0.25
Outputs:
- layer_out: bfloat16 [8192, 1024], P(('user', 'item'))
- token_grad: bfloat16 [16384, 1024], P(('user', 'item'))
- item_grad: float32 [1024, 1024], P('item', 'user')
Inputs may be any that keep to these rules, and one draw needn't show every extreme that they name: `lengths`: A device's histories lie in its rows in order from row 0 and fill at most 512 rows; every destination receives a history of exactly 64 tokens. `destination`: A device sends its 8 histories to 8 different destinations along user; the histories sent to one device by the devices of its item index, placed at their worker_offset, cover its 256 rows exactly once. `positives`: the target ids of a device lie among the 256 table rows of its item index. `negatives`: columns k * 64 to k * 64 + 63 of each group name rows held by item index k.
All inputs are finite; a program needn't handle non-finite values.
Results may differ from a plain program's by a relative error of at most 0.017.
Values may be sent and summed in bfloat16 or wider, within the bound.
A program may use at most 64 MiB of HBM per device.

v0:
```python
import jax
import jax.numpy as jnp
from jax import lax
from jax.sharding import PartitionSpec as P

HEAD = 128
TOK_DEV = 256
norm_epsilon = 1e-05
scale_epsilon = 1e-06
inverse_temp = 20.0
loss_scale = 32.0


def layer_norm(values, gain):
    center = jnp.mean(values, axis=-1, keepdims=True)
    shifted = values - center
    spread = jnp.mean(shifted * shifted, axis=-1, keepdims=True)
    return shifted * lax.rsqrt(spread + norm_epsilon) * gain


def hstu_block(rows, segment, in_gain, w_uvqk, out_gain, w_out):
    count = rows.shape[0]
    rows_f = rows.astype(jnp.float32)
    normed = layer_norm(rows_f, in_gain).astype(jnp.bfloat16)
    projected = jnp.dot(
        normed,
        lax.all_gather(w_uvqk, "item", axis=0, tiled=True),
        preferred_element_type=jnp.float32,
    )
    active = jax.nn.silu(projected).astype(jnp.bfloat16)
    width = active.shape[1] // 4
    heads = width // HEAD
    gate_u = active[:, :width]
    values_v = active[:, width : 2 * width].reshape(count, heads, HEAD)
    queries = active[:, 2 * width : 3 * width].reshape(count, heads, HEAD)
    key_rows = active[:, 3 * width :].reshape(count, heads, HEAD)
    scores = jnp.einsum(
        "qhd,khd->hqk", queries, key_rows, preferred_element_type=jnp.float32
    ) * HEAD ** (-0.5)
    order = jnp.arange(count, dtype=jnp.int32)
    allowed = (segment[:, None] == segment[None, :]) & (order[None, :] <= order[:, None])
    weights = jnp.where(allowed[None], jax.nn.silu(scores), 0.0).astype(jnp.bfloat16)
    mixed = jnp.einsum(
        "hqk,khd->qhd", weights, values_v, preferred_element_type=jnp.float32
    ).reshape(count, width)
    gated = (layer_norm(mixed, out_gain) * gate_u.astype(jnp.float32)).astype(jnp.bfloat16)
    delta = jnp.dot(
        gated, lax.all_gather(w_out, "item", axis=1, tiled=True), preferred_element_type=jnp.float32
    )
    return (rows_f + delta).astype(jnp.bfloat16)


def dispatch(rows, home_start, history_len, targets, offsets, slot_rows, user_count):
    peers = jnp.arange(user_count, dtype=jnp.int32)
    chosen = (targets[None, :] == peers[:, None]).astype(jnp.int32)
    first_row = jnp.sum(chosen * home_start[None, :], axis=1)
    sent_count = jnp.sum(chosen * history_len[None, :], axis=1)
    landing = jnp.sum(chosen * offsets[None, :], axis=1)
    within = jnp.arange(slot_rows, dtype=jnp.int32)
    picked = jnp.minimum(first_row[:, None] + within[None, :], rows.shape[0] - 1)
    filled = within[None, :] < sent_count[:, None]
    parcels = jnp.where(filled[:, :, None], rows[picked], jnp.zeros((), rows.dtype))
    labels = jnp.stack([landing, sent_count], axis=1)
    arrived, arrived_labels = (
        lax.all_to_all(parcels, "user", split_axis=0, concat_axis=0, tiled=True),
        lax.all_to_all(labels, "user", split_axis=0, concat_axis=0, tiled=True),
    )
    worker_rows = jnp.arange(TOK_DEV, dtype=jnp.int32)
    lower = arrived_labels[:, 0]
    upper = lower + arrived_labels[:, 1]
    inside = (
        (worker_rows[:, None] >= lower[None, :]) & (worker_rows[:, None] < upper[None, :])
    ).astype(jnp.int32)
    source = jnp.sum(inside * peers[None, :], axis=1)
    begin = jnp.sum(inside * lower[None, :], axis=1)
    flattened = arrived.reshape(-1, arrived.shape[-1])
    gathered = flattened[source * slot_rows + worker_rows - begin]
    return (gathered, source, arrived_labels)


def per_device(
    tokens,
    lengths,
    destination,
    worker_offset,
    positives,
    negatives,
    table,
    in_gain,
    w_uvqk,
    out_gain,
    w_out,
):
    user_count = lax.axis_size("user")
    item_count = lax.axis_size("item")
    item_here = lax.axis_index("item")
    user_here = lax.axis_index("user")
    home_rows = tokens.shape[0]
    model_width = tokens.shape[1]
    hist_count = lengths.shape[1]
    slot_rows = home_rows // hist_count
    history_len = lengths[0]
    targets = destination[0]
    offsets = worker_offset[0]
    home_start = jnp.cumsum(history_len) - history_len
    row_ids = jnp.arange(home_rows, dtype=jnp.int32)
    finished = (row_ids[:, None] >= (home_start + history_len)[None, :]).astype(jnp.int32)
    home_segment = jnp.sum(finished, axis=1)
    valid = row_ids < jnp.sum(history_len)
    home_out = hstu_block(tokens, home_segment, in_gain, w_uvqk, out_gain, w_out)
    layer_out = dispatch(
        home_out, home_start, history_len, targets, offsets, slot_rows, user_count
    )[0]
    item_rows = table.shape[0]
    table_f = table.astype(jnp.float32)
    table_scale = lax.rsqrt(jnp.mean(table_f * table_f, axis=1) + scale_epsilon)
    table_hat = table_f * table_scale[:, None]
    table_low = table_hat.astype(jnp.bfloat16)
    share = negatives.shape[1] // item_count
    owned_ids = (
        lax.dynamic_slice_in_dim(negatives, item_here * share, share, 1) - item_here * item_rows
    )
    group_rows = lax.all_to_all(
        table_low[owned_ids], "item", split_axis=0, concat_axis=0, tiled=True
    ).reshape(-1, model_width)
    positive_local = positives - item_here * item_rows
    positive_rows = table_low[positive_local]
    out_f = home_out.astype(jnp.float32)
    out_scale = lax.rsqrt(jnp.mean(out_f * out_f, axis=1) + scale_epsilon)
    out_hat = out_f * out_scale[:, None]
    out_low = out_hat.astype(jnp.bfloat16)
    factor = inverse_temp / model_width
    positive_logit = (
        jnp.einsum("rd,rd->r", out_low, positive_rows, preferred_element_type=jnp.float32) * factor
    )
    negative_logit = (
        jnp.einsum("rd,nd->rn", out_low, group_rows, preferred_element_type=jnp.float32) * factor
    )
    positive_exp = jnp.exp(positive_logit)
    negative_exp = jnp.exp(negative_logit)
    partition = positive_exp + jnp.sum(negative_exp, axis=1)
    weight = jnp.where(valid, loss_scale, 0.0)
    positive_grad = weight * (positive_exp / partition - 1.0)
    negative_grad = (weight[:, None] * negative_exp / partition[:, None]).astype(jnp.bfloat16)
    grad_hat = (
        positive_grad[:, None] * positive_rows.astype(jnp.float32)
        + jnp.dot(negative_grad, group_rows, preferred_element_type=jnp.float32)
    ) * factor
    token_grad = (
        (grad_hat - out_hat * jnp.mean(grad_hat * out_hat, axis=1, keepdims=True))
        * out_scale[:, None]
    ).astype(jnp.bfloat16)
    negative_terms = (
        jnp.einsum("rn,rd->nd", negative_grad, out_low, preferred_element_type=jnp.float32) * factor
    )
    owned_terms = lax.all_to_all(
        negative_terms.reshape(item_count, share, model_width).astype(jnp.bfloat16),
        "item",
        split_axis=0,
        concat_axis=0,
        tiled=True,
    ).astype(jnp.float32)
    positive_terms = (positive_grad * factor)[:, None] * out_low.astype(jnp.float32)
    catalog = jnp.arange(item_rows, dtype=jnp.int32)
    positive_hits = (positive_local[None, :] == catalog[:, None]).astype(jnp.float32)
    negative_hits = (owned_ids.reshape(-1)[None, :] == catalog[:, None]).astype(jnp.float32)
    row_sums = jnp.dot(positive_hits, positive_terms, precision=lax.Precision.HIGHEST)
    row_sums = row_sums + jnp.dot(
        negative_hits, owned_terms.reshape(-1, model_width), precision=lax.Precision.HIGHEST
    )
    column_width = model_width // user_count
    totals = lax.psum(row_sums.astype(jnp.bfloat16), "user").astype(jnp.float32)
    inner = jnp.mean(totals * table_hat, axis=1)
    whole = (totals - table_hat * inner[:, None]) * table_scale[:, None]
    item_grad = lax.dynamic_slice_in_dim(whole, user_here * column_width, column_width, 1)
    return (layer_out, token_grad, item_grad)


def solution(mesh):
    return jax.shard_map(
        per_device,
        mesh=mesh,
        in_specs=(
            P(("user", "item"), None),
            P(("user", "item"), None),
            P(("user", "item"), None),
            P(("user", "item"), None),
            P(("user", "item")),
            P(),
            P("item", None),
            P(),
            P("item", None),
            P(),
            P(None, "item"),
        ),
        out_specs=(P(("user", "item"), None), P(("user", "item"), None), P("item", "user")),
        check_vma=False,
    )
```

profile of v0, /device:TPU:0, one launch (start us, length us, event | category | flops | bytes accessed | tf_op | source)
XLA Modules:
  0.0 229.4 jit_solution(2644495984975450326)
XLA Ops:
  7.2 0.7 all-gather.3.cloned.1.call-update
  7.9 0.8 reduce-window.4
  8.8 1.4 fusion.62
  10.1 0.8 select_reduce_fusion.2
  11.0 0.7 copy.32
  11.7 5.2 %all-to-all-start.1 = ((s32[8,1,2]{2,1,0:T(1,128)}), s32[8,1,2]{2,1,0:T(1,128)S(1)}, u32[]{:S(2)}, u32[]{:S(2)}) async-start(s32[8,1,2]{2,1,0:T(1,128)} %copy.32), calls=%async_computation.1 | async-start | bytes 8192 | tf_op jit(solution)/shard_map/all_to_all | solution.py:66
  16.9 0.7 all-gather.5.cloned.1.call-update
  17.7 1.5 convert_reduce_fusion
  19.2 0.4 fusion.5
  19.7 0.1 convert_reduce_fusion.1
  19.8 0.2 fusion.34
  20.0 0.2 fusion.23
  20.2 0.2 fusion.58
  20.5 0.1 reshape.277
  20.6 2.0 gather_fusion.2
  22.6 2.0 gather_fusion.3
  24.6 0.7 fusion.52
  25.6 4.9 %all-to-all-start.2 = ((bf16[4,64,1024]{2,1,0:T(8,128)(2,1)}), bf16[4,64,1024]{2,1,0:T(8,128)(2,1)S(1)}, u32[]{:S(2)}, u32[]{:S(2)}) async-start(bf16[4,64,1024]{2,1,0:T(8,128)(2,1)} %bitcast.67), calls=%async_computation.2 | async-start | bytes 1048576 | tf_op jit(solution)/shard_map/all_to_all | solution.py:123
  30.5 0.1 select_reduce_fusion.1
  30.6 73.6 %all-gather.3.cloned.1.call-done = bf16[1024,2048]{1,0:T(8,128)(2,1)} async-done(((bf16[256,2048]{1,0:T(8,128)(2,1)}), bf16[1024,2048]{1,0:T(8,128)(2,1)}) %all-gather.3.cloned.1.call-update) | async-done | bytes 4194320 | tf_op jit(solution)/shard_map/all_gather | solution.py:27
  104.2 5.1 %multiply_convert_fusion = bf16[512,2048]{1,0:T(8,128)(2,1)S(1)} fusion(bf16[1024,2048]{1,0:T(8,128)(2,1)} %all-gather.3.cloned.1.call-done, bf16[512,1024]{1,0:T(8,128)(2,1)S(1)} %copy-done.1, f32[1024]{0:T(1024)S(1)} %copy-done.8, f32[512]{0:T(512)S(1)} %add_rsqrt_fusion.2, f32[512]{0:T(512)S(1)} %broadcast_multiply_fusion.3), kind=kOutput, calls=%fused_computation.5 | convolution fusion | flops 2155347968 | bytes 7348224 | tf_op jit(solution)/shard_map/dot_general | solution.py:25
  109.3 1.3 copy-done.3
  110.6 1.2 slice_bitcast_fusion.1
  111.8 1.0 copy.38
  112.8 3.4 %fusion.63 = (f32[512]{0:T(512)S(1)}, f32[4,128,512]{2,1,0:T(8,128)S(1)}) fusion(bf16[512,4,128]{0,2,1:T(8,128)(2,1)} %bitcast.72, pred[512,512]{1,0:T(8,128)(4,1)S(1)} %fusion.34, bf16[64,4,8,128]{3,2,1,0:T(8,128)(2,1)} %get-tuple-element.15, bf16[64,4,8,128]{3,2,1,0:T(8,128)(2,1)} %get-tuple-element.14), kind=kOutput, calls=%fused_computation.121 | convolution fusion | flops 544472576 | bytes 2885632 | tf_op jit(solution)/shard_map/hqk,khd->qhd/dot_general | solution.py:43
  116.2 1.3 copy.39
  117.5 0.2 fusion.29
  117.7 16.4 %all-gather.5.cloned.1.call-done = bf16[512,1024]{1,0:T(8,128)(2,1)} async-done(((bf16[512,256]{1,0:T(8,128)(2,1)}), bf16[512,1024]{1,0:T(8,128)(2,1)}) %all-gather.5.cloned.1.call-update) | async-done | bytes 1048592 | tf_op jit(solution)/shard_map/all_gather | solution.py:48
  134.1 3.0 %fusion.12 = (f32[512]{0:T(512)S(1)}, bf16[512,1024]{1,0:T(8,128)(2,1)S(1)}) fusion(bf16[512,1024]{1,0:T(8,128)(2,1)} %all-gather.5.cloned.1.call-done, f32[512,512]{1,0:T(8,128)} %copy.39, bf16[512,2048]{1,0:T(8,128)(2,1)} %copy-done.3, f32[512]{0:T(512)S(1)} %copy-done.9, f32[512]{0:T(512)S(1)} %add_rsqrt_fusion.1, f32[512]{0:T(512)S(1)} %broadcast_multiply_fusion.1, ...), kind=kOutput, calls=%fused_computation.26 | convolution fusion | flops 541588992 | bytes 4726784 | tf_op jit(solution)/shard_map/dot_general | solution.py:47
  137.1 0.5 fusion.15
  137.6 0.6 fusion.68
  138.2 0.7 broadcast_multiply_fusion
  139.0 1.3 fusion.20
  140.3 3.8 %all-to-all-start.3 = ((bf16[4,64,1024]{2,1,0:T(8,128)(2,1)}), bf16[4,64,1024]{2,1,0:T(8,128)(2,1)S(1)}, u32[]{:S(2)}, u32[]{:S(2)}) async-start(bf16[4,64,1024]{2,1,0:T(8,128)(2,1)} %bitcast.71), calls=%async_computation.3 | async-start | bytes 1048576 | tf_op jit(solution)/shard_map/all_to_all | solution.py:156
  144.2 2.8 %gather_fusion = bf16[512,1024]{1,0:T(8,128)(2,1)} fusion(bf16[512,1024]{1,0:T(8,128)(2,1)S(1)} %get-tuple-element.25, s32[1024]{0:T(1024)S(1)} %pad_clamp_fusion.3), kind=kCustom, calls=%fused_computation | custom fusion | bytes 2099200 | tf_op jit(solution)/shard_map/gather | solution.py:62
  147.0 2.4 %broadcast_select_fusion = bf16[8,64,1024]{2,1,0:T(8,128)(2,1)} fusion(bf16[8,64,1024]{2,1,0:T(8,128)(2,1)} %bitcast.65, pred[8,64]{1,0:T(8,128)(4,1)S(1)} %iota_compare_fusion.9), kind=kLoop, calls=%fused_computation.54 | loop fusion | flops 524288 | bytes 2097664 | tf_op jit(solution)/shard_map/jit(_where)/select_n | solution.py:62
  149.4 2.1 fusion.8
  151.5 5.7 %all-to-all-done.3 = bf16[4,64,1024]{2,1,0:T(8,128)(2,1)S(1)} async-done(((bf16[4,64,1024]{2,1,0:T(8,128)(2,1)}), bf16[4,64,1024]{2,1,0:T(8,128)(2,1)S(1)}, u32[]{:S(2)}, u32[]{:S(2)}) %all-to-all-start.3) | async-done | bytes 524320 | tf_op jit(solution)/shard_map/all_to_all | solution.py:156
  157.2 4.2 %all-to-all-start = ((bf16[8,64,1024]{2,1,0:T(8,128)(2,1)}), bf16[8,64,1024]{2,1,0:T(8,128)(2,1)S(1)}, u32[]{:S(2)}, u32[]{:S(2)}) async-start(bf16[8,64,1024]{2,1,0:T(8,128)(2,1)} %broadcast_select_fusion), calls=%async_computation | async-start | bytes 2097152 | tf_op jit(solution)/shard_map/all_to_all | solution.py:65
  161.5 0.3 fusion.48
  161.8 2.4 %fusion.21 = bf16[256,1024]{1,0:T(8,128)(2,1)} fusion(f32[256,1024]{1,0:T(8,128)S(1)} %fusion.48, f32[512]{0:T(512)S(1)} %get-tuple-element.8, s32[512]{0:T(512)S(1)} %get-tuple-element.13, bf16[512,1024]{1,0:T(8,128)(2,1)S(1)} %get-tuple-element.25, f32[512]{0:T(512)S(1)} %add_rsqrt_fusion), kind=kOutput, calls=%fused_computation.38 | convolution fusion | flops 1613889536 | bytes 2627584 | tf_op jit(solution)/shard_map/dot_general | solution.py:167
  164.2 3.0 %fusion.11 = bf16[512,1024]{1,0:T(8,128)(2,1)} fusion(f32[512,1024]{1,0:T(8,128)} %get-tuple-element.29, bf16[512,1024]{1,0:T(8,128)(2,1)S(1)} %get-tuple-element.25, f32[512]{0:T(512)S(1)} %broadcast_multiply_fusion.2, f32[512]{0:T(512)S(1)} %add_rsqrt_fusion), kind=kLoop, calls=%fused_computation.25 | loop fusion | flops 3145728 | bytes 4198400 | tf_op jit(solution)/shard_map/convert_element_type | solution.py:152
  167.2 11.0 %all-to-all-done = bf16[8,64,1024]{2,1,0:T(8,128)(2,1)S(1)} async-done(((bf16[8,64,1024]{2,1,0:T(8,128)(2,1)}), bf16[8,64,1024]{2,1,0:T(8,128)(2,1)S(1)}, u32[]{:S(2)}, u32[]{:S(2)}) %all-to-all-start) | async-done | bytes 1048608 | tf_op jit(solution)/shard_map/all_to_all | solution.py:65
  178.2 2.0 gather_fusion.1
  180.2 40.3 %all-reduce.2.cloned.1.call-done = bf16[256,1024]{1,0:T(8,128)(2,1)} async-done(((bf16[256,1024]{1,0:T(8,128)(2,1)}), bf16[256,1024]{1,0:T(8,128)(2,1)}) %all-reduce.2.cloned.1.call-update) | async-done | bytes 524304 | tf_op jit(solution)/shard_map/psum | solution.py:172
  220.5 1.4 multiply_reduce_fusion
  221.9 0.1 convert_element_type.84
  222.0 0.8 fusion.49
  (53 shorter events, 0.9 us)
Async XLA Ops:
  7.2 12.1 %copy-start.1 = (bf16[512,1024]{1,0:T(8,128)(2,1)S(1)}, bf16[512,1024]{1,0:T(8,128)(2,1)}, u32[]{:S(2)}) copy-start(bf16[512,1024]{1,0:T(8,128)(2,1)} %param.11) | copy-start | bytes 3145732
  7.2 12.8 %copy-start.6 = (s32[512]{0:T(512)S(1)}, s32[512]{0:T(512)}, u32[]{:S(2)}) copy-start(s32[512]{0:T(512)} %param.15) | copy-start | bytes 6148
  7.2 12.8 %copy-start = (bf16[256,1024]{1,0:T(8,128)(2,1)S(1)}, bf16[256,1024]{1,0:T(8,128)(2,1)}, u32[]{:S(2)}) copy-start(bf16[256,1024]{1,0:T(8,128)(2,1)} %param.17) | copy-start | bytes 1572868
  7.2 97.0 %all-gather.3.cloned.1.call-start = ((), (), s32[]{:S(2)}) async-start(), calls=%async_computation.4 | async-start | bytes 5242880 | tf_op jit(solution)/shard_map/all_gather | solution.py:27
  11.7 13.9 %all-to-all-start.1 = ((s32[8,1,2]{2,1,0:T(1,128)}), s32[8,1,2]{2,1,0:T(1,128)S(1)}, u32[]{:S(2)}, u32[]{:S(2)}) async-start(s32[8,1,2]{2,1,0:T(1,128)} %copy.32), calls=%async_computation.1 | async-start | bytes 8192 | tf_op jit(solution)/shard_map/all_to_all | solution.py:66
  16.9 3.5 %copy-start.7 = (s32[4,256]{1,0:T(4,128)S(1)}, s32[4,256]{1,0:T(4,128)}, u32[]{:S(2)}) copy-start(s32[4,256]{1,0:T(4,128)} %param.16) | copy-start | bytes 12292
  16.9 117.2 %all-gather.5.cloned.1.call-start = ((), (), s32[]{:S(2)}) async-start(), calls=%async_computation.5 | async-start | bytes 1310720 | tf_op jit(solution)/shard_map/all_gather | solution.py:48
  22.6 81.6 %copy-start.8 = (f32[1024]{0:T(1024)S(1)}, f32[1024]{0:T(1024)}, u32[]{:S(2)}) copy-start(f32[1024]{0:T(1024)} %param.18) | copy-start | bytes 12292
  25.6 112.0 %all-to-all-start.2 = ((bf16[4,64,1024]{2,1,0:T(8,128)(2,1)}), bf16[4,64,1024]{2,1,0:T(8,128)(2,1)S(1)}, u32[]{:S(2)}, u32[]{:S(2)}) async-start(bf16[4,64,1024]{2,1,0:T(8,128)(2,1)} %bitcast.67), calls=%async_computation.2 | async-start | bytes 1048576 | tf_op jit(solution)/shard_map/all_to_all | solution.py:123
  109.3 1.4 copy-start.3
  116.2 17.9 %copy-start.9 = (f32[512]{0:T(512)S(1)}, f32[512]{0:T(512)}, u32[]{:S(2)}) copy-start(f32[512]{0:T(512)} %param.20) | copy-start | bytes 6148
  137.6 2.7 %copy-start.4 = (bf16[4,64,1024]{2,1,0:T(8,128)(2,1)}, bf16[4,64,1024]{2,1,0:T(8,128)(2,1)S(1)}, u32[]{:S(2)}) copy-start(bf16[4,64,1024]{2,1,0:T(8,128)(2,1)S(1)} %all-to-all-done.2) | copy-start | bytes 1572868
  138.2 0.8 copy-start.10
  140.3 16.9 %all-to-all-start.3 = ((bf16[4,64,1024]{2,1,0:T(8,128)(2,1)}), bf16[4,64,1024]{2,1,0:T(8,128)(2,1)S(1)}, u32[]{:S(2)}, u32[]{:S(2)}) async-start(bf16[4,64,1024]{2,1,0:T(8,128)(2,1)} %bitcast.71), calls=%async_computation.3 | async-start | bytes 1048576 | tf_op jit(solution)/shard_map/all_to_all | solution.py:156
  147.0 2.4 %copy-start.5 = (bf16[4,64,1024]{2,1,0:T(8,128)(2,1)S(1)}, bf16[4,64,1024]{2,1,0:T(8,128)(2,1)}, u32[]{:S(2)}) copy-start(bf16[4,64,1024]{2,1,0:T(8,128)(2,1)} %copy-done.4) | copy-start | bytes 1572868
  147.0 2.4 %copy-start.11 = (f32[512,256]{0,1:T(8,128)S(1)}, f32[512,256]{0,1:T(8,128)}, u32[]{:S(2)}) copy-start(f32[512,256]{0,1:T(8,128)} %copy-done.10) | copy-start | bytes 1572868
  157.2 21.0 %all-to-all-start = ((bf16[8,64,1024]{2,1,0:T(8,128)(2,1)}), bf16[8,64,1024]{2,1,0:T(8,128)(2,1)S(1)}, u32[]{:S(2)}, u32[]{:S(2)}) async-start(bf16[8,64,1024]{2,1,0:T(8,128)(2,1)} %broadcast_select_fusion), calls=%async_computation | async-start | bytes 2097152 | tf_op jit(solution)/shard_map/all_to_all | solution.py:65
  161.5 59.0 %all-reduce.2.cloned.1.call-start = ((), (), s32[]{:S(2)}) async-start(), calls=%async_computation.6 | async-start | bytes 1048576 | tf_op jit(solution)/shard_map/psum | solution.py:172
  220.5 1.4 copy-start.2
Sparse Core Ops, SparseCore 0:
  9.6 94.5 all-gather.2
  105.7 28.3 all-gather.4
  165.4 55.0 all-reduce.1
where the time goes:
time: 230 us; the launch traced here: 229 us
  waiting for transfers between devices  148 us (64%)
  starting transfers between devices  18.2 us (8%)
  matrix products  18.1 us (8%)
  other arithmetic  15.9 us (7%)
  local copies, waits for them, and re-layouts  14.7 us (6%)
  between operations  14 us (6%)
    all_gather x1, waiting for transfers between devices, hstu_block(): lax.all_gather(w_uvqk, 'item', axis=0, tiled=True)  73.6 us
    psum x1, waiting for transfers between devices, per_device(): totals = lax.psum(row_sums.astype(jnp.bfloat16), 'user').astype(jnp.float32)  40.3 us
    all_gather x1, waiting for transfers between devices, hstu_block(): lax.all_gather(w_out, 'item', axis=1, tiled=True)  16.4 us
    all_to_all x1, waiting for transfers between devices, dispatch(): lax.all_to_all(parcels, 'user', split_axis=0, concat_axis=0, tiled=True)  11 us
    all_to_all x1, waiting for transfers between devices, per_device(): lax.all_to_all(negative_terms.reshape(item_count, share, model_width).ast...  5.72 us
    all_to_all x1, starting transfers between devices, dispatch(): lax.all_to_all(labels, 'user', split_axis=0, concat_axis=0, tiled=True)  5.2 us
    dot_general x1, matrix products, hstu_block(): jnp.dot(normed, lax.all_gather(w_uvqk, 'item', axis=0, tiled=True), prefe...  5.07 us
    all_to_all x1, starting transfers between devices, per_device(): lax.all_to_all(table_low[owned_ids], 'item', split_axis=0, concat_axis=0,...  4.85 us
  transfers between devices with their start and end apart: 7, of which 5 were waited for; matrix products, arithmetic and copies ran while one was open for 18% of the time, Pallas kernels for 0%

commit v1 on v0

--- a/solution.py
+++ b/solution.py
@@ -24,7 +24,9 @@
     normed = layer_norm(rows_f, in_gain).astype(jnp.bfloat16)
     projected = jnp.dot(
         normed,
-        lax.all_gather(w_uvqk, "item", axis=0, tiled=True),
+        jnp.concatenate(
+            lax.all_to_all(jnp.stack([w_uvqk] * lax.axis_size("item")), "item", 0, 0), axis=0
+        ),
         preferred_element_type=jnp.float32,
     )
     active = jax.nn.silu(projected).astype(jnp.bfloat16)

time: 230 us -> 253 us (1.10)
  waiting for transfers between devices: 148 us -> 161 us
  blocking collectives: 0 us -> 9.68 us
  local copies, waits for them, and re-layouts: 14.7 us -> 17.9 us
    all_to_all x1, waiting for transfers between devices: 0.01 us -> 103 us  [hstu_block(): lax.all_to_all(jnp.stack([w_uvqk] * lax.axis_size('item')), 'item', 0, 0)]
    all_gather x1 -> x0, waiting for transfers between devices: 73.6 us -> none  [hstu_block(): lax.all_gather(w_uvqk, 'item', axis=0, tiled=True)]
    all_gather x1, waiting for transfers between devices: 16.4 us -> 0.01 us  [hstu_block(): lax.all_gather(w_out, 'item', axis=1, tiled=True)]
    all_to_all x0 -> x1, blocking collectives: none -> 9.68 us  [dispatch(): lax.all_to_all(labels, 'user', split_axis=0, concat_axis=0, tiled=True)]
    another operation x0 -> x1, local copies, waits for them, and re-layouts: none -> 3.73 us  [hstu_block(): jnp.stack([w_uvqk] * lax.axis_size('item'))]
  transfers between devices with their start and end apart: 7 -> 6, of which waited for: 5 -> 4; matrix products, arithmetic and copies ran while one was open for 18% -> 15% of each run, Pallas kernels for 0% -> 0%
where the time goes in v1:
time: 253 us; the launch traced here: 252 us
  waiting for transfers between devices  161 us (64%)
  matrix products  18.1 us (7%)
  local copies, waits for them, and re-layouts  17.9 us (7%)
  starting transfers between devices  17.2 us (7%)
  other arithmetic  14.4 us (6%)
  between operations  14.3 us (6%)
  blocking collectives  9.68 us (4%)
    all_to_all x1, waiting for transfers between devices, hstu_block(): lax.all_to_all(jnp.stack([w_uvqk] * lax.axis_size('item')), 'item', 0, 0)  103 us
    psum x1, waiting for transfers between devices, per_device(): totals = lax.psum(row_sums.astype(jnp.bfloat16), 'user').astype(jnp.float32)  40.3 us
    all_to_all x1, waiting for transfers between devices, dispatch(): lax.all_to_all(parcels, 'user', split_axis=0, concat_axis=0, tiled=True)  10.9 us
    all_to_all x1, blocking collectives, dispatch(): lax.all_to_all(labels, 'user', split_axis=0, concat_axis=0, tiled=True)  9.68 us
    all_to_all x1, waiting for transfers between devices, per_device(): lax.all_to_all(negative_terms.reshape(item_count, share, model_width).ast...  6.06 us
    all_to_all x1, starting transfers between devices, per_device(): lax.all_to_all(negative_terms.reshape(item_count, share, model_width).ast...  5.1 us
  transfers between devices with their start and end apart: 6, of which 4 were waited for; matrix products, arithmetic and copies ran while one was open for 15% of the time, Pallas kernels for 0%

profile of v1, /device:TPU:0, one launch (start us, length us, event | category | flops | bytes accessed | tf_op | source)
XLA Modules:
  0.0 252.4 jit_solution(4557234465850791253)
XLA Ops:
  7.2 0.8 reduce-window.4
  8.0 1.3 fusion.62
  9.3 0.8 select_reduce_fusion.2
  10.2 9.7 %all_to_all.32 = s32[8,1,2]{2,1,0:T(1,128)S(1)} all-to-all(s32[8,1,2]{2,1,0:T(1,128)S(1)} %copy.32), channel_id=1, replica_groups=mesh['user'=8,'item'=4] {'user'}, dimensions={0} | all-to-all | bytes 128 | tf_op jit(solution)/shard_map/all_to_all | solution.py:68
  19.9 3.7 %stack.6 = bf16[4,256,2048]{2,1,0:T(8,128)(2,1)} broadcast(bf16[256,2048]{1,0:T(8,128)(2,1)} %param.19), dimensions={1,2} | broadcast | bytes 5242880 | tf_op jit(solution)/shard_map/stack | solution.py:28
  23.6 5.0 %all-to-all-start = ((bf16[4,256,2048]{2,1,0:T(8,128)(2,1)}), bf16[4,256,2048]{2,1,0:T(8,128)(2,1)}, u32[]{:S(2)}, u32[]{:S(2)}) async-start(bf16[4,256,2048]{2,1,0:T(8,128)(2,1)} %stack.6), calls=%async_computation | async-start | bytes 8388608 | tf_op jit(solution)/shard_map/all_to_all | solution.py:28
  28.7 0.7 all-gather.2.cloned.1.call-update
  29.5 0.1 reshape.283
  29.6 0.2 fusion.23
  29.8 0.2 fusion.58
  29.9 2.1 gather_fusion.2
  32.0 2.0 gather_fusion.3
  34.2 0.6 fusion.52
  34.9 0.1 convert_reduce_fusion.1
  35.0 0.2 convert_reduce_fusion
  35.2 0.4 fusion.5
  35.7 0.2 fusion.34
  36.0 0.1 select_reduce_fusion.1
  36.1 102.8 %all-to-all-done = bf16[4,256,2048]{2,1,0:T(8,128)(2,1)} async-done(((bf16[4,256,2048]{2,1,0:T(8,128)(2,1)}), bf16[4,256,2048]{2,1,0:T(8,128)(2,1)}, u32[]{:S(2)}, u32[]{:S(2)}) %all-to-all-start) | async-done | bytes 4194336 | tf_op jit(solution)/shard_map/all_to_all | solution.py:28
  138.9 3.5 %all-to-all-start.3 = ((bf16[4,64,1024]{2,1,0:T(8,128)(2,1)}), bf16[4,64,1024]{2,1,0:T(8,128)(2,1)S(1)}, u32[]{:S(2)}, u32[]{:S(2)}) async-start(bf16[4,64,1024]{2,1,0:T(8,128)(2,1)} %bitcast.22), calls=%async_computation.3 | async-start | bytes 1048576 | tf_op jit(solution)/shard_map/all_to_all | solution.py:125
  142.4 5.1 %multiply_convert_fusion = bf16[512,2048]{1,0:T(8,128)(2,1)S(1)} fusion(bf16[1024,2048]{1,0:T(8,128)(2,1)} %bitcast.2, bf16[512,1024]{1,0:T(8,128)(2,1)S(1)} %copy-done.1, f32[1024]{0:T(1024)S(1)} %copy-done.8, f32[512]{0:T(512)S(1)} %add_rsqrt_fusion.2, f32[512]{0:T(512)S(1)} %broadcast_multiply_fusion.3), kind=kOutput, calls=%fused_computation.5 | convolution fusion | flops 2155347968 | bytes 7348224 | tf_op jit(solution)/shard_map/dot_general | solution.py:25
  147.5 1.3 copy-done.3
  148.8 1.2 slice_bitcast_fusion.1
  150.0 1.0 copy.38
  151.0 3.4 %fusion.63 = (f32[512]{0:T(512)S(1)}, f32[4,128,512]{2,1,0:T(8,128)S(1)}) fusion(bf16[512,4,128]{0,2,1:T(8,128)(2,1)} %bitcast.72, pred[512,512]{1,0:T(8,128)(4,1)S(1)} %fusion.34, bf16[64,4,8,128]{3,2,1,0:T(8,128)(2,1)} %get-tuple-element.15, bf16[64,4,8,128]{3,2,1,0:T(8,128)(2,1)} %get-tuple-element.14), kind=kOutput, calls=%fused_computation.121 | convolution fusion | flops 544472576 | bytes 2885632 | tf_op jit(solution)/shard_map/hqk,khd->qhd/dot_general | solution.py:45
  154.5 1.3 copy.39
  155.8 0.2 fusion.29
  156.0 3.0 %fusion.12 = (f32[512]{0:T(512)S(1)}, bf16[512,1024]{1,0:T(8,128)(2,1)S(1)}) fusion(bf16[512,1024]{1,0:T(8,128)(2,1)} %all-gather.2.cloned.1.call-done, f32[512,512]{1,0:T(8,128)} %copy.39, bf16[512,2048]{1,0:T(8,128)(2,1)} %copy-done.3, f32[512]{0:T(512)S(1)} %copy-done.9, f32[512]{0:T(512)S(1)} %add_rsqrt_fusion.1, f32[512]{0:T(512)S(1)} %broadcast_multiply_fusion.1, ...), kind=kOutput, calls=%fused_computation.26 | convolution fusion | flops 541588992 | bytes 4726784 | tf_op jit(solution)/shard_map/dot_general | solution.py:49
  158.9 0.5 fusion.15
  159.5 0.6 fusion.68
  160.1 0.7 broadcast_multiply_fusion
  160.8 0.1 copy-done.10
  160.9 1.3 fusion.20
  162.2 5.1 %all-to-all-start.4 = ((bf16[4,64,1024]{2,1,0:T(8,128)(2,1)}), bf16[4,64,1024]{2,1,0:T(8,128)(2,1)S(1)}, u32[]{:S(2)}, u32[]{:S(2)}) async-start(bf16[4,64,1024]{2,1,0:T(8,128)(2,1)} %bitcast.71), calls=%async_computation.4 | async-start | bytes 1048576 | tf_op jit(solution)/shard_map/all_to_all | solution.py:158
  167.3 2.8 %gather_fusion = bf16[512,1024]{1,0:T(8,128)(2,1)} fusion(bf16[512,1024]{1,0:T(8,128)(2,1)S(1)} %get-tuple-element.25, s32[1024]{0:T(1024)S(1)} %pad_clamp_fusion.3), kind=kCustom, calls=%fused_computation | custom fusion | bytes 2099200 | tf_op jit(solution)/shard_map/gather | solution.py:64
  170.1 2.4 broadcast_select_fusion
  172.6 2.1 fusion.8
  174.6 6.1 %all-to-all-done.4 = bf16[4,64,1024]{2,1,0:T(8,128)(2,1)S(1)} async-done(((bf16[4,64,1024]{2,1,0:T(8,128)(2,1)}), bf16[4,64,1024]{2,1,0:T(8,128)(2,1)S(1)}, u32[]{:S(2)}, u32[]{:S(2)}) %all-to-all-start.4) | async-done | bytes 524320 | tf_op jit(solution)/shard_map/all_to_all | solution.py:158
  180.7 3.6 %all-to-all-start.1 = ((bf16[8,64,1024]{2,1,0:T(8,128)(2,1)}), bf16[8,64,1024]{2,1,0:T(8,128)(2,1)S(1)}, u32[]{:S(2)}, u32[]{:S(2)}) async-start(bf16[8,64,1024]{2,1,0:T(8,128)(2,1)} %broadcast_select_fusion), calls=%async_computation.1 | async-start | bytes 2097152 | tf_op jit(solution)/shard_map/all_to_all | solution.py:67
  184.3 0.3 fusion.48
  184.6 2.4 fusion.21
  187.1 3.0 %fusion.11 = bf16[512,1024]{1,0:T(8,128)(2,1)} fusion(f32[512,1024]{1,0:T(8,128)} %get-tuple-element.29, bf16[512,1024]{1,0:T(8,128)(2,1)S(1)} %get-tuple-element.25, f32[512]{0:T(512)S(1)} %broadcast_multiply_fusion.2, f32[512]{0:T(512)S(1)} %add_rsqrt_fusion), kind=kLoop, calls=%fused_computation.25 | loop fusion | flops 3145728 | bytes 4198400 | tf_op jit(solution)/shard_map/convert_element_type | solution.py:154
  190.1 10.9 %all-to-all-done.1 = bf16[8,64,1024]{2,1,0:T(8,128)(2,1)S(1)} async-done(((bf16[8,64,1024]{2,1,0:T(8,128)(2,1)}), bf16[8,64,1024]{2,1,0:T(8,128)(2,1)S(1)}, u32[]{:S(2)}, u32[]{:S(2)}) %all-to-all-start.1) | async-done | bytes 1048608 | tf_op jit(solution)/shard_map/all_to_all | solution.py:67
  201.0 2.0 gather_fusion.1
  203.0 40.3 %all-reduce.2.cloned.1.call-done = bf16[256,1024]{1,0:T(8,128)(2,1)} async-done(((bf16[256,1024]{1,0:T(8,128)(2,1)}), bf16[256,1024]{1,0:T(8,128)(2,1)}) %all-reduce.2.cloned.1.call-update) | async-done | bytes 524304 | tf_op jit(solution)/shard_map/psum | solution.py:174
  243.2 1.4 multiply_reduce_fusion
  244.7 0.1 convert_element_type.84
  244.8 0.8 fusion.49
  (52 shorter events, 0.8 us)
Async XLA Ops:
  23.6 5.7 %copy-start.7 = (s32[4,256]{1,0:T(4,128)S(1)}, s32[4,256]{1,0:T(4,128)}, u32[]{:S(2)}) copy-start(s32[4,256]{1,0:T(4,128)} %param.16) | copy-start | bytes 12292
  23.6 5.9 %copy-start.6 = (s32[512]{0:T(512)S(1)}, s32[512]{0:T(512)}, u32[]{:S(2)}) copy-start(s32[512]{0:T(512)} %param.15) | copy-start | bytes 6148
  23.6 5.9 %copy-start = (bf16[256,1024]{1,0:T(8,128)(2,1)S(1)}, bf16[256,1024]{1,0:T(8,128)(2,1)}, u32[]{:S(2)}) copy-start(bf16[256,1024]{1,0:T(8,128)(2,1)} %param.17) | copy-start | bytes 1572868
  23.6 115.3 %all-to-all-start = ((bf16[4,256,2048]{2,1,0:T(8,128)(2,1)}), bf16[4,256,2048]{2,1,0:T(8,128)(2,1)}, u32[]{:S(2)}, u32[]{:S(2)}) async-start(bf16[4,256,2048]{2,1,0:T(8,128)(2,1)} %stack.6), calls=%async_computation | async-start | bytes 8388608 | tf_op jit(solution)/shard_map/all_to_all | solution.py:28
  28.6 127.3 %all-gather.2.cloned.1.call-start = ((), (), s32[]{:S(2)}) async-start(), calls=%async_computation.5 | async-start | bytes 1310720 | tf_op jit(solution)/shard_map/all_gather | solution.py:50
  32.0 3.0 %copy-start.1 = (bf16[512,1024]{1,0:T(8,128)(2,1)S(1)}, bf16[512,1024]{1,0:T(8,128)(2,1)}, u32[]{:S(2)}) copy-start(bf16[512,1024]{1,0:T(8,128)(2,1)} %param.11) | copy-start | bytes 3145732
  34.0 108.4 %copy-start.8 = (f32[1024]{0:T(1024)S(1)}, f32[1024]{0:T(1024)}, u32[]{:S(2)}) copy-start(f32[1024]{0:T(1024)} %param.18) | copy-start | bytes 12292
  138.9 20.5 %all-to-all-start.3 = ((bf16[4,64,1024]{2,1,0:T(8,128)(2,1)}), bf16[4,64,1024]{2,1,0:T(8,128)(2,1)S(1)}, u32[]{:S(2)}, u32[]{:S(2)}) async-start(bf16[4,64,1024]{2,1,0:T(8,128)(2,1)} %bitcast.22), calls=%async_computation.3 | async-start | bytes 1048576 | tf_op jit(solution)/shard_map/all_to_all | solution.py:125
  147.5 1.4 copy-start.3
  154.4 1.5 copy-start.9
  159.5 2.7 %copy-start.4 = (bf16[4,64,1024]{2,1,0:T(8,128)(2,1)}, bf16[4,64,1024]{2,1,0:T(8,128)(2,1)S(1)}, u32[]{:S(2)}) copy-start(bf16[4,64,1024]{2,1,0:T(8,128)(2,1)S(1)} %all-to-all-done.3) | copy-start | bytes 1572868
  160.1 0.8 copy-start.10
  162.2 18.5 %all-to-all-start.4 = ((bf16[4,64,1024]{2,1,0:T(8,128)(2,1)}), bf16[4,64,1024]{2,1,0:T(8,128)(2,1)S(1)}, u32[]{:S(2)}, u32[]{:S(2)}) async-start(bf16[4,64,1024]{2,1,0:T(8,128)(2,1)} %bitcast.71), calls=%async_computation.4 | async-start | bytes 1048576 | tf_op jit(solution)/shard_map/all_to_all | solution.py:158
  170.1 2.4 copy-start.5
  170.1 2.4 copy-start.11
  180.7 20.3 %all-to-all-start.1 = ((bf16[8,64,1024]{2,1,0:T(8,128)(2,1)}), bf16[8,64,1024]{2,1,0:T(8,128)(2,1)S(1)}, u32[]{:S(2)}, u32[]{:S(2)}) async-start(bf16[8,64,1024]{2,1,0:T(8,128)(2,1)} %broadcast_select_fusion), calls=%async_computation.1 | async-start | bytes 2097152 | tf_op jit(solution)/shard_map/all_to_all | solution.py:67
  184.3 59.0 %all-reduce.2.cloned.1.call-start = ((), (), s32[]{:S(2)}) async-start(), calls=%async_computation.6 | async-start | bytes 1048576 | tf_op jit(solution)/shard_map/psum | solution.py:174
  243.2 1.4 copy-start.2
Sparse Core Ops, SparseCore 0:
  31.0 53.3 all-gather.1
  188.2 55.0 all-reduce.1
